TPU v7x, 32 devices: a whole 2x2x4 slice. The times are simulated.
32 devices in a mesh: dom: 16 (over z, y, x), blk: 2 (over core).
Axes of the slice: x: 2, y: 2, z: 4, core: 2. Of those that a mesh axis runs over, the one named last changes fastest.
Arguments:
- self_block: float32 [96, 96, 4096], P(None, None, ('dom', 'blk')), may hold values from -1 to 8
- couple: float32 [64, 96, 4096], P(None, None, ('dom', 'blk')), may hold values from -0.625 to 0.625
- inverse: float32 [64, 64, 4096], P(None, None, ('dom', 'blk')), may hold values from -1 to 8
- body_force: float32 [3, 64, 4096], P(None, None, ('dom', 'blk')), may hold values from -6 to 6
- face_mortar: int32 [24576], P(('dom', 'blk')), may hold values from 0 to 8191, as said below
- face_kind: int32 [24576], P(('dom', 'blk')), may hold values from 0 to 4
Outputs:
- trace_field: float32 [48, 8192], P(None, ('dom', 'blk'))
- interior: float32 [3, 64, 4096], P(None, None, ('dom', 'blk'))
Inputs may be any that keep to these rules, and one draw needn't show every extreme that they name: `face_mortar`: mortar m is owned by device m // 256 along the curve. The 768 slots of device r come in five runs in this order: mortars owned by r - 2, r - 1, r, r + 1, r + 32 // 2 (modulo 32); each of the four other runs holds 1 to 32 slots and one of them holds exactly 32; the first 256 slots of the run owned by r name each of r's mortars once.
All inputs are finite; a program needn't handle non-finite values.
Results may differ from a plain program's by a relative error of at most 0.0003.
Values sent between devices are 32-bit elements; how exact they have to be, the bound alone decides.
No kernel may reach another device: no remote copies, remote signals or barrier semaphores. Data moves between devices by JAX's collectives and lax.ppermute only.
A program may use at most 128 MiB of HBM per device.

v0:
```python
import jax
import jax.numpy as jnp
import numpy as np
from jax import lax
from jax.sharding import PartitionSpec as P

ITERS = 3
PRECISE = lax.Precision.HIGHEST


def near_offsets(ranks):
    return (-2, -1, 1, ranks // 2)


def interp_tables():
    abscissae = -np.cos(np.pi * np.arange(4) / 3.0)

    def lagrange(points):
        columns = [
            np.prod(
                [
                    (points - abscissae[other_node])
                    / (abscissae[basis_node] - abscissae[other_node])
                    for other_node in range(4)
                    if other_node != basis_node
                ],
                axis=0,
            )
            for basis_node in range(4)
        ]
        return np.stack(columns, axis=1)

    lower_map = lagrange((abscissae - 1.0) / 2.0)
    upper_map = lagrange((abscissae + 1.0) / 2.0)
    identity = np.eye(4)
    return np.stack(
        [
            np.kron(identity, identity),
            np.kron(lower_map, lower_map),
            np.kron(lower_map, upper_map),
            np.kron(upper_map, lower_map),
            np.kron(upper_map, upper_map),
        ]
    )


def to_faces(values, kind_ids, tables):
    node_count = tables.shape[1]
    by_comp = values.reshape(values.shape[0] // node_count, node_count, values.shape[1])
    mapped = jnp.einsum("kab,cbi->kcai", tables, by_comp, precision=PRECISE)
    selector = (kind_ids[None, :] == jnp.arange(5, dtype=jnp.int32)[:, None]).astype(values.dtype)
    return jnp.einsum("kcai,ki->cai", mapped, selector, precision=PRECISE).reshape(values.shape)


def to_mortar(values, kind_ids, tables):
    node_count = tables.shape[1]
    by_comp = values.reshape(values.shape[0] // node_count, node_count, values.shape[1])
    mapped = jnp.einsum("kab,cai->kcbi", tables, by_comp, precision=PRECISE)
    selector = (kind_ids[None, :] == jnp.arange(5, dtype=jnp.int32)[:, None]).astype(values.dtype)
    return jnp.einsum("kcbi,ki->cbi", mapped, selector, precision=PRECISE).reshape(values.shape)


def slot_to_element(values, elements, node_count):
    comp_count = values.shape[0] // node_count
    arranged = values.reshape(comp_count, node_count, elements, 6)
    return jnp.transpose(arranged, (0, 3, 1, 2)).reshape(comp_count, 6 * node_count, elements)


def element_to_slot(values, elements, node_count):
    comp_count = values.shape[0]
    arranged = values.reshape(comp_count, 6, node_count, elements)
    return jnp.transpose(arranged, (0, 2, 3, 1)).reshape(comp_count * node_count, elements * 6)


def to_owners(buffer):
    result = lax.all_to_all(buffer, ("dom", "blk"), split_axis=1, concat_axis=1, tiled=True)
    return result


def to_elements(buffer):
    result = lax.all_to_all(buffer, ("dom", "blk"), split_axis=1, concat_axis=1, tiled=True)
    return result


def local(self_block, couple, inverse, body_force, face_mortar, face_kind):
    elements = self_block.shape[2]
    owned = 2 * elements
    capacity = max(2, elements // 4)
    ranks = lax.axis_size(("dom", "blk"))
    offsets_list = near_offsets(ranks)
    my_rank = lax.axis_index(("dom", "blk"))
    tables = jnp.asarray(interp_tables(), dtype=jnp.float32)
    node_count = tables.shape[1]
    owner_rank = face_mortar // owned
    local_index = face_mortar % owned
    distance = (owner_rank - my_rank) % ranks
    offset = jnp.where(distance > ranks // 2, distance - ranks, distance)
    is_self = offset == 0
    slot_ids = jnp.arange(face_mortar.shape[0], dtype=jnp.int32)
    run_start = jnp.zeros_like(slot_ids)
    run_block = jnp.zeros_like(slot_ids)
    for number in range(len(offsets_list)):
        shift_by = offsets_list[number]
        inside = offset == shift_by
        run_start = jnp.where(inside, jnp.sum((offset < shift_by).astype(jnp.int32)), run_start)
        run_block = jnp.where(inside, number, run_block)
    position = slot_ids - run_start
    buffer_width = ranks * capacity
    target = (my_rank + offset) % ranks * capacity + position
    target = jnp.where(is_self, buffer_width, target)
    sent_index = (
        jnp.full((buffer_width + 1,), owned, jnp.int32).at[target].set(local_index)[:buffer_width]
    )
    readers = lax.all_to_all(sent_index, ("dom", "blk"), split_axis=0, concat_axis=0, tiled=True)
    all_index = jnp.concatenate([jnp.where(is_self, local_index, owned), readers])
    column = jnp.where(is_self, local_index, owned + target)

    def assemble(per_element):
        slot_values = element_to_slot(per_element, elements, node_count)
        mortar_values = to_mortar(slot_values, face_kind, tables)
        outgoing = (
            jnp.zeros((mortar_values.shape[0], buffer_width + 1), jnp.float32)
            .at[:, target]
            .set(mortar_values)[:, :buffer_width]
        )
        received = to_owners(outgoing)
        stacked = jnp.concatenate([mortar_values, received], axis=1)
        return (
            jnp.zeros((mortar_values.shape[0], owned + 1), jnp.float32)
            .at[:, all_index]
            .add(stacked)[:, :owned]
        )

    def spread(field_values):
        padded = jnp.concatenate(
            [field_values, jnp.zeros((field_values.shape[0], 1), jnp.float32)], axis=1
        )
        received = to_elements(padded[:, readers])
        source = jnp.concatenate([field_values, received], axis=1)
        return slot_to_element(to_faces(source[:, column], face_kind, tables), elements, node_count)

    solved_load = jnp.einsum("ike,cke->cie", inverse, body_force, precision=PRECISE)
    local_rhs = jnp.einsum("iae,cie->cae", couple, solved_load, precision=PRECISE)
    residual = assemble(local_rhs)
    weighted = jnp.einsum("ike,kbe->ibe", inverse, couple, precision=PRECISE)
    condensed = self_block + jnp.einsum("iae,ibe->abe", couple, weighted, precision=PRECISE)
    trace_field = jnp.zeros_like(residual)
    direction = residual
    current = lax.psum(jnp.sum(residual * residual), ("dom", "blk"))
    for iteration in range(ITERS):
        image_field = assemble(
            jnp.einsum("abe,cbe->cae", condensed, spread(direction), precision=PRECISE)
        )
        curve_sum, cross_sum, image_sum = lax.psum(
            (
                jnp.sum(direction * image_field),
                jnp.sum(residual * image_field),
                jnp.sum(image_field * image_field),
            ),
            ("dom", "blk"),
        )
        step_length = current / curve_sum
        trace_field = trace_field + step_length * direction
        if iteration + 1 < ITERS:
            residual = residual - step_length * image_field
            following = (
                current - 2.0 * step_length * cross_sum + step_length * step_length * image_sum
            )
            direction = residual + following / current * direction
            current = following
    faces_elem = spread(trace_field)
    difference = body_force - jnp.einsum("ibe,cbe->cie", couple, faces_elem, precision=PRECISE)
    interior = jnp.einsum("ike,cke->cie", inverse, difference, precision=PRECISE)
    return (trace_field, interior)


def solution(mesh):
    placed = (
        P(None, None, ("dom", "blk")),
        P(None, None, ("dom", "blk")),
        P(None, None, ("dom", "blk")),
        P(None, None, ("dom", "blk")),
        P(("dom", "blk")),
        P(("dom", "blk")),
    )
    return jax.shard_map(
        local,
        mesh=mesh,
        in_specs=placed,
        out_specs=(P(None, ("dom", "blk")), P(None, None, ("dom", "blk"))),
        check_vma=False,
    )
```

profile of v0, /device:TPU:1, one launch (start us, length us, event | category | flops | bytes accessed | tf_op | source)
XLA Modules:
  0.0 478.3 jit_solution(3439235943275158686)
XLA Ops:
  9.6 7.1 %all-to-all-start = ((s32[32,32,1]{1,2,0:T(1,128)}), s32[32,32,1]{1,2,0:T(1,128)S(1)}, u32[]{:S(2)}, u32[]{:S(2)}) async-start(s32[32,32,1]{1,2,0:T(1,128)} %bitcast.16), calls=%async_computation | async-start | bytes 32768 | tf_op jit(solution)/shard_map/all_to_all | solution.py:114
  28.0 8.5 %convolution_bitcast_fusion.14 = f32[3,64,128]{1,0,2:T(4,128)S(1)} fusion(f32[3,64,128]{1,0,2:T(4,128)S(1)} %copy.376, f32[64,64,128]{1,0,2:T(8,128)} %copy.377), kind=kOutput, calls=%fused_computation.55 | convolution fusion | flops 18874368 | bytes 2293760 | tf_op jit(solution)/shard_map/ike,cke->cie/dot_general | solution.py:142
  36.5 7.2 %fusion.54 = f32[128,96,64]{1,2,0:T(8,128)} fusion(f32[64,96,128]{1,0,2:T(8,128)S(1)} %copy-done, f32[64,64,128]{1,0,2:T(8,128)} %copy.377), kind=kOutput, calls=%fused_computation.135 | convolution fusion | flops 603979776 | bytes 8388608 | tf_op jit(solution)/shard_map/ike,kbe->ibe/dot_general | solution.py:145
  48.2 14.5 %fusion = f32[128,96,96]{2,1,0:T(8,128)} fusion(f32[64,96,128]{1,0,2:T(8,128)} %copy.378, f32[128,96,64]{1,2,0:T(8,128)} %fusion.54), kind=kOutput, calls=%fused_computation.18 | convolution fusion | flops 905969664 | bytes 11010048 | tf_op jit(solution)/shard_map/iae,ibe->abe/dot_general | solution.py:146
  83.3 7.9 %all-to-all-done.1 = f32[32,1,1536]{2,1,0:T(1,128)S(1)} async-done(((f32[32,1,1536]{2,1,0:T(1,128)}), f32[32,1,1536]{2,1,0:T(1,128)S(1)}, u32[]{:S(2)}, u32[]{:S(2)}) %all-to-all-start.1) | async-done | bytes 196640 | tf_op jit(solution)/shard_map/all_to_all | solution.py:76
  93.6 13.1 %scatter_custom_fusion.2 = f32[48,257]{0,1:T(8,128)S(1)} fusion(s32[1792]{0:T(1024)S(1)} %fusion.42, f32[1792,48]{1,0:T(8,128)S(1)} %copy.384, f32[]{:T(128)} %constant.68.clone.1), kind=kCustom, calls=%fused_computation.91 | custom fusion | flops 86016 | bytes 49348 | tf_op jit(solution)/shard_map/scatter-add | solution.py:131
  113.5 7.0 %bitcast_add_fusion = f32[96,96,128]{2,1,0:T(8,128)} fusion(f32[96,96,128]{2,1,0:T(8,128)} %param.7, f32[128,96,96]{0,1,2:T(8,128)} %copy.393), kind=kLoop, calls=%fused_computation.17 | loop fusion | flops 1179648 | bytes 14155776 | tf_op jit(solution)/shard_map/add | solution.py:146
  131.8 11.8 %convolution_bitcast_fusion.12 = f32[3,96,128]{1,0,2:T(4,128)S(1)} fusion(f32[3,96,128]{1,0,2:T(4,128)S(1)} %copy.394, f32[96,96,128]{1,0,2:T(8,128)} %copy.395), kind=kOutput, calls=%fused_computation.53 | convolution fusion | flops 42467328 | bytes 5013504 | tf_op jit(solution)/shard_map/abe,cbe->cae/dot_general | solution.py:152
  150.9 15.3 %all_to_all.105 = f32[32,1,1536]{2,1,0:T(1,128)S(1)} all-to-all(f32[32,1,1536]{2,1,0:T(1,128)S(1)} %reshape.405), channel_id=1, replica_groups=mesh['dom'=16,'blk'=2] {'dom','blk'}, dimensions={0} | all-to-all | bytes 393216 | tf_op jit(solution)/shard_map/all_to_all | solution.py:76
  168.0 13.1 %scatter_custom_fusion.4 = f32[48,257]{0,1:T(8,128)S(1)} fusion(s32[1792]{0:T(1024)S(1)} %fusion.42, f32[1792,48]{1,0:T(8,128)S(1)} %copy.401, f32[]{:T(128)} %constant.68.clone.1), kind=kCustom, calls=%fused_computation.88 | custom fusion | flops 86016 | bytes 49348 | tf_op jit(solution)/shard_map/scatter-add | solution.py:131
  181.9 37.7 %all-reduce.4 = (f32[]{:T(128)}, f32[]{:T(128)}, f32[]{:T(128)}) all-reduce(f32[]{:T(128)} %get-tuple-element.23, f32[]{:T(128)} %get-tuple-element.22, f32[]{:T(128)} %get-tuple-element.21), channel_id=1, replica_groups=mesh['dom'=16,'blk'=2] {'dom','blk'}, use_global_device_ids=true, to_apply=%region_8.9 | all-reduce | flops 3 | bytes 24 | tf_op jit(solution)/shard_map/psum | solution.py:149
  226.9 13.9 %all_to_all.106 = f32[32,1,1536]{2,1,0:T(1,128)S(1)} all-to-all(f32[32,1,1536]{2,1,0:T(1,128)S(1)} %reshape.407), channel_id=1, replica_groups=mesh['dom'=16,'blk'=2] {'dom','blk'}, dimensions={0} | all-to-all | bytes 393216 | tf_op jit(solution)/shard_map/all_to_all | solution.py:81
  245.8 11.8 %convolution_bitcast_fusion.11 = f32[3,96,128]{1,0,2:T(4,128)S(1)} fusion(f32[3,96,128]{1,0,2:T(4,128)S(1)} %copy.407, f32[96,96,128]{1,0,2:T(8,128)} %copy.395), kind=kOutput, calls=%fused_computation.52 | convolution fusion | flops 42467328 | bytes 5013504 | tf_op jit(solution)/shard_map/abe,cbe->cae/dot_general | solution.py:152
  264.9 11.6 %all_to_all.107 = f32[32,1,1536]{2,1,0:T(1,128)S(1)} all-to-all(f32[32,1,1536]{2,1,0:T(1,128)S(1)} %reshape.409), channel_id=1, replica_groups=mesh['dom'=16,'blk'=2] {'dom','blk'}, dimensions={0} | all-to-all | bytes 393216 | tf_op jit(solution)/shard_map/all_to_all | solution.py:76
  278.3 13.1 %scatter_custom_fusion.6 = f32[48,257]{0,1:T(8,128)S(1)} fusion(s32[1792]{0:T(1024)S(1)} %fusion.42, f32[1792,48]{1,0:T(8,128)S(1)} %copy.414, f32[]{:T(128)} %constant.68.clone.1), kind=kCustom, calls=%fused_computation.86 | custom fusion | flops 86016 | bytes 49348 | tf_op jit(solution)/shard_map/scatter-add | solution.py:131
  292.2 37.7 %all-reduce.3 = (f32[]{:T(128)}, f32[]{:T(128)}, f32[]{:T(128)}) all-reduce(f32[]{:T(128)} %get-tuple-element.20, f32[]{:T(128)} %get-tuple-element.19, f32[]{:T(128)} %get-tuple-element.18), channel_id=1, replica_groups=mesh['dom'=16,'blk'=2] {'dom','blk'}, use_global_device_ids=true, to_apply=%region_18.19 | all-reduce | flops 3 | bytes 24 | tf_op jit(solution)/shard_map/psum | solution.py:154
  335.3 13.9 %all_to_all.108 = f32[32,1,1536]{2,1,0:T(1,128)S(1)} all-to-all(f32[32,1,1536]{2,1,0:T(1,128)S(1)} %reshape.411), channel_id=1, replica_groups=mesh['dom'=16,'blk'=2] {'dom','blk'}, dimensions={0} | all-to-all | bytes 393216 | tf_op jit(solution)/shard_map/all_to_all | solution.py:81
  354.2 11.8 %convolution_bitcast_fusion.10 = f32[3,96,128]{1,0,2:T(4,128)S(1)} fusion(f32[3,96,128]{1,0,2:T(4,128)S(1)} %copy.420, f32[96,96,128]{1,0,2:T(8,128)} %copy.395), kind=kOutput, calls=%fused_computation.51 | convolution fusion | flops 42467328 | bytes 5013504 | tf_op jit(solution)/shard_map/abe,cbe->cae/dot_general | solution.py:152
  373.3 11.6 %all_to_all.109 = f32[32,1,1536]{2,1,0:T(1,128)S(1)} all-to-all(f32[32,1,1536]{2,1,0:T(1,128)S(1)} %reshape.413), channel_id=1, replica_groups=mesh['dom'=16,'blk'=2] {'dom','blk'}, dimensions={0} | all-to-all | bytes 393216 | tf_op jit(solution)/shard_map/all_to_all | solution.py:76
  386.8 13.1 %scatter_custom_fusion.8 = f32[48,257]{0,1:T(8,128)S(1)} fusion(s32[1792]{0:T(1024)S(1)} %fusion.42, f32[1792,48]{1,0:T(8,128)S(1)} %copy.427, f32[]{:T(128)} %constant.68.clone.1), kind=kCustom, calls=%fused_computation.84 | custom fusion | flops 86016 | bytes 49348 | tf_op jit(solution)/shard_map/scatter-add | solution.py:131
  400.6 37.6 %psum.58 = f32[]{:T(128)} all-reduce(f32[]{:T(128)} %fusion.31), channel_id=1, replica_groups=mesh['dom'=16,'blk'=2] {'dom','blk'}, use_global_device_ids=true, to_apply=%region_26.27 | all-reduce | flops 1 | bytes 8 | tf_op jit(solution)/shard_map/psum | solution.py:154
  448.5 8.5 %all-to-all-done.8 = f32[32,1,1536]{2,1,0:T(1,128)S(1)} async-done(((f32[32,1,1536]{2,1,0:T(1,128)}), f32[32,1,1536]{2,1,0:T(1,128)S(1)}, u32[]{:S(2)}, u32[]{:S(2)}) %all-to-all-start.8) | async-done | bytes 196640 | tf_op jit(solution)/shard_map/all_to_all | solution.py:81
  462.1 8.5 %fusion.22 = f32[3,64,128]{1,0,2:T(4,128)S(1)} fusion(f32[3,64,128]{1,0,2:T(4,128)S(1)} %copy-done.4, f32[3,96,128]{1,0,2:T(4,128)S(1)} %copy.433, f32[64,96,128]{1,0,2:T(8,128)} %copy.378), kind=kOutput, calls=%fused_computation.50 | convolution fusion | flops 28336128 | bytes 3489792 | tf_op jit(solution)/shard_map/ibe,cbe->cie/dot_general | solution.py:172
  470.6 6.6 %convolution_bitcast_fusion.8 = f32[3,64,128]{1,0,2:T(4,128)S(1)} fusion(f32[3,64,128]{1,0,2:T(4,128)S(1)} %fusion.22, f32[64,64,128]{1,0,2:T(8,128)S(1)} %copy-done.1), kind=kOutput, calls=%fused_computation.48 | convolution fusion | flops 18874368 | bytes 2293760 | tf_op jit(solution)/shard_map/ike,cke->cie/dot_general | solution.py:173
  (152 shorter events, 126.8 us)
Async XLA Ops:
  0.6 22.9 %copy-start.5 = (f32[64,64,128]{2,1,0:T(8,128)S(1)}, f32[64,64,128]{2,1,0:T(8,128)}, u32[]{:S(2)}) copy-start(f32[64,64,128]{2,1,0:T(8,128)} %param.9) | copy-start | bytes 6291460
  9.6 66.6 %all-to-all-start = ((s32[32,32,1]{1,2,0:T(1,128)}), s32[32,32,1]{1,2,0:T(1,128)S(1)}, u32[]{:S(2)}, u32[]{:S(2)}) async-start(s32[32,32,1]{1,2,0:T(1,128)} %bitcast.16), calls=%async_computation | async-start | bytes 32768 | tf_op jit(solution)/shard_map/all_to_all | solution.py:114
  18.4 9.6 %copy-start.3 = (f32[3,64,128]{1,0,2:T(4,128)}, f32[3,64,128]{1,0,2:T(4,128)S(1)}, u32[]{:S(2)}) copy-start(f32[3,64,128]{1,0,2:T(4,128)S(1)} %copy.376) | copy-start | bytes 294916
  28.0 8.5 %copy-start = (f32[64,96,128]{1,0,2:T(8,128)S(1)}, f32[64,96,128]{1,0,2:T(8,128)}, u32[]{:S(2)}) copy-start(f32[64,96,128]{1,0,2:T(8,128)} %copy.378) | copy-start | bytes 9437188
  48.2 14.5 %copy-start.2 = (f32[5,16,16,1]{1,2,0,3:T(8,128)S(1)}, f32[5,16,16,1]{1,2,0,3:T(8,128)}, u32[]{:S(2)}) copy-start(f32[5,16,16,1]{1,2,0,3:T(8,128)} %constant.104) | copy-start | bytes 15364
  76.1 30.6 %copy-start.6 = (pred[257]{0:T(512)(128)(4,1)S(1)}, pred[257]{0:T(512)(128)(4,1)}, u32[]{:S(2)}) copy-start(pred[257]{0:T(512)(128)(4,1)} %constant.86.clone.1) | copy-start | bytes 775
  76.1 15.1 %all-to-all-start.1 = ((f32[32,1,1536]{2,1,0:T(1,128)}), f32[32,1,1536]{2,1,0:T(1,128)S(1)}, u32[]{:S(2)}, u32[]{:S(2)}) async-start(f32[32,1,1536]{2,1,0:T(1,128)} %reshape.401), calls=%async_computation.1 | async-start | bytes 393216 | tf_op jit(solution)/shard_map/all_to_all | solution.py:76
  110.9 15.9 %all-to-all-start.2 = ((f32[32,1,1536]{2,1,0:T(1,128)}), f32[32,1,1536]{2,1,0:T(1,128)S(1)}, u32[]{:S(2)}, u32[]{:S(2)}) async-start(f32[32,1,1536]{2,1,0:T(1,128)} %reshape.403), calls=%async_computation.2 | async-start | bytes 393216 | tf_op jit(solution)/shard_map/all_to_all | solution.py:81
  442.9 14.1 %all-to-all-start.8 = ((f32[32,1,1536]{2,1,0:T(1,128)}), f32[32,1,1536]{2,1,0:T(1,128)S(1)}, u32[]{:S(2)}, u32[]{:S(2)}) async-start(f32[32,1,1536]{2,1,0:T(1,128)} %reshape.415), calls=%async_computation.8 | async-start | bytes 393216 | tf_op jit(solution)/shard_map/all_to_all | solution.py:81
  458.5 3.6 copy-start.4
  462.1 8.5 %copy-start.1 = (f32[64,64,128]{1,0,2:T(8,128)S(1)}, f32[64,64,128]{1,0,2:T(8,128)}, u32[]{:S(2)}) copy-start(f32[64,64,128]{1,0,2:T(8,128)} %copy.377) | copy-start | bytes 6291460
where the time goes:
time: 488 us; the launch traced here: 478 us
  blocking collectives  179 us (37%)
  matrix products  93.1 us (19%)
  local copies, waits for them, and re-layouts  83.2 us (17%)
  other arithmetic  77.3 us (16%)
  starting transfers between devices  20.5 us (4%)
  waiting for transfers between devices  16.4 us (3%)
  between operations  8.46 us (2%)
    psum x2, blocking collectives, local(): lax.psum((jnp.sum(direction * image_field), jnp.sum(residual * image_fiel...  75.3 us
    scatter-add x4, other arithmetic, assemble(): return jnp.zeros((mortar_values.shape[0], owned + 1), jnp.float32).at[:,...  52.6 us
    all_to_all x3, blocking collectives, to_owners(): lax.all_to_all(buffer, ('dom', 'blk'), split_axis=1, concat_axis=1, tiled...  38.5 us
    psum x1, blocking collectives, local(): current = lax.psum(jnp.sum(residual * residual), ('dom', 'blk'))  37.7 us
    dot_general x3, matrix products, local(): jnp.einsum('abe,cbe->cae', condensed, spread(direction), precision=PRECISE)  35.5 us
    all_to_all x2, blocking collectives, to_elements(): lax.all_to_all(buffer, ('dom', 'blk'), split_axis=1, concat_axis=1, tiled...  27.9 us
    unnamed x36, local copies, waits for them, and re-layouts  20 us
    scatter x4, local copies, waits for them, and re-layouts, assemble(): outgoing = jnp.zeros((mortar_values.shape[0], buffer_width + 1), jnp.floa...  17.1 us
  transfers between devices with their start and end apart: 4, of which 2 were waited for; matrix products, arithmetic and copies ran while one was open for 16% of the time, Pallas kernels for 0%

commit v1 on v0

--- a/solution.py
+++ b/solution.py
@@ -151,13 +151,13 @@
         image_field = assemble(
             jnp.einsum("abe,cbe->cae", condensed, spread(direction), precision=PRECISE)
         )
-        curve_sum, cross_sum, image_sum = lax.psum(
+        rest_hubs = lambda xx: lax.psum(lax.psum(xx, axis_name="blk"), axis_name="dom")
+        curve_sum, cross_sum, image_sum = rest_hubs(
             (
                 jnp.sum(direction * image_field),
                 jnp.sum(residual * image_field),
                 jnp.sum(image_field * image_field),
-            ),
-            ("dom", "blk"),
+            )
         )
         step_length = current / curve_sum
         trace_field = trace_field + step_length * direction

time: 488 us -> 533 us (1.092)
  blocking collectives: 179 us -> 220 us
    psum x2 -> x6, blocking collectives: 75.3 us -> 108 us  [the longest x3 97.3 us: local(): lax.psum(lax.psum(xx, axis_name='blk'), axis_name='dom')]
    all_to_all x2, blocking collectives: 27.9 us -> 36.5 us  [to_elements(): lax.all_to_all(buffer, ('dom', 'blk'), split_axis=1, concat_axis=1, tiled...]
  transfers between devices with their start and end apart: 4 -> 4, of which waited for: 2 -> 2; matrix products, arithmetic and copies ran while one was open for 16% -> 14% of each run, Pallas kernels for 0% -> 0%
where the time goes in v1:
time: 533 us; the launch traced here: 524 us
  blocking collectives  220 us (41%)
  matrix products  93.1 us (17%)
  local copies, waits for them, and re-layouts  83.2 us (16%)
  other arithmetic  77.3 us (15%)
  starting transfers between devices  25.3 us (5%)
  waiting for transfers between devices  16.6 us (3%)
  between operations  8.29 us (2%)
    psum x3, blocking collectives, local(): lax.psum(lax.psum(xx, axis_name='blk'), axis_name='dom')  97.3 us
    scatter-add x4, other arithmetic, assemble(): return jnp.zeros((mortar_values.shape[0], owned + 1), jnp.float32).at[:,...  52.6 us
    all_to_all x3, blocking collectives, to_owners(): lax.all_to_all(buffer, ('dom', 'blk'), split_axis=1, concat_axis=1, tiled...  38.3 us
    psum x1, blocking collectives, local(): current = lax.psum(jnp.sum(residual * residual), ('dom', 'blk'))  37.6 us
    all_to_all x2, blocking collectives, to_elements(): lax.all_to_all(buffer, ('dom', 'blk'), split_axis=1, concat_axis=1, tiled...  36.5 us
    dot_general x3, matrix products, local(): jnp.einsum('abe,cbe->cae', condensed, spread(direction), precision=PRECISE)  35.5 us
    unnamed x36, local copies, waits for them, and re-layouts  20 us
    scatter x4, local copies, waits for them, and re-layouts, assemble(): outgoing = jnp.zeros((mortar_values.shape[0], buffer_width + 1), jnp.floa...  17.1 us
  transfers between devices with their start and end apart: 4, of which 2 were waited for; matrix products, arithmetic and copies ran while one was open for 14% of the time, Pallas kernels for 0%

profile of v1, /device:TPU:1, one launch (start us, length us, event | category | flops | bytes accessed | tf_op | source)
XLA Modules:
  0.0 523.7 jit_solution(13813557679346247300)
XLA Ops:
  9.6 7.1 %all-to-all-start = ((s32[32,32,1]{1,2,0:T(1,128)}), s32[32,32,1]{1,2,0:T(1,128)S(1)}, u32[]{:S(2)}, u32[]{:S(2)}) async-start(s32[32,32,1]{1,2,0:T(1,128)} %bitcast.16), calls=%async_computation | async-start | bytes 32768 | tf_op jit(solution)/shard_map/all_to_all | solution.py:114
  28.0 8.5 %convolution_bitcast_fusion.14 = f32[3,64,128]{1,0,2:T(4,128)S(1)} fusion(f32[3,64,128]{1,0,2:T(4,128)S(1)} %copy.376, f32[64,64,128]{1,0,2:T(8,128)} %copy.377), kind=kOutput, calls=%fused_computation.55 | convolution fusion | flops 18874368 | bytes 2293760 | tf_op jit(solution)/shard_map/ike,cke->cie/dot_general | solution.py:142
  36.5 7.2 %fusion.54 = f32[128,96,64]{1,2,0:T(8,128)} fusion(f32[64,96,128]{1,0,2:T(8,128)S(1)} %copy-done, f32[64,64,128]{1,0,2:T(8,128)} %copy.377), kind=kOutput, calls=%fused_computation.135 | convolution fusion | flops 603979776 | bytes 8388608 | tf_op jit(solution)/shard_map/ike,kbe->ibe/dot_general | solution.py:145
  48.2 14.5 %fusion = f32[128,96,96]{2,1,0:T(8,128)} fusion(f32[64,96,128]{1,0,2:T(8,128)} %copy.378, f32[128,96,64]{1,2,0:T(8,128)} %fusion.54), kind=kOutput, calls=%fused_computation.18 | convolution fusion | flops 905969664 | bytes 11010048 | tf_op jit(solution)/shard_map/iae,ibe->abe/dot_general | solution.py:146
  83.3 7.9 %all-to-all-done.1 = f32[32,1,1536]{2,1,0:T(1,128)S(1)} async-done(((f32[32,1,1536]{2,1,0:T(1,128)}), f32[32,1,1536]{2,1,0:T(1,128)S(1)}, u32[]{:S(2)}, u32[]{:S(2)}) %all-to-all-start.1) | async-done | bytes 196640 | tf_op jit(solution)/shard_map/all_to_all | solution.py:76
  93.6 13.1 %scatter_custom_fusion.2 = f32[48,257]{0,1:T(8,128)S(1)} fusion(s32[1792]{0:T(1024)S(1)} %fusion.42, f32[1792,48]{1,0:T(8,128)S(1)} %copy.384, f32[]{:T(128)} %constant.68.clone.1), kind=kCustom, calls=%fused_computation.91 | custom fusion | flops 86016 | bytes 49348 | tf_op jit(solution)/shard_map/scatter-add | solution.py:131
  131.8 11.8 %convolution_bitcast_fusion.12 = f32[3,96,128]{1,0,2:T(4,128)S(1)} fusion(f32[3,96,128]{1,0,2:T(4,128)S(1)} %copy.394, f32[96,96,128]{1,0,2:T(8,128)} %copy.395), kind=kOutput, calls=%fused_computation.53 | convolution fusion | flops 42467328 | bytes 5013504 | tf_op jit(solution)/shard_map/abe,cbe->cae/dot_general | solution.py:152
  150.9 15.3 %all_to_all.105 = f32[32,1,1536]{2,1,0:T(1,128)S(1)} all-to-all(f32[32,1,1536]{2,1,0:T(1,128)S(1)} %reshape.405), channel_id=1, replica_groups=mesh['dom'=16,'blk'=2] {'dom','blk'}, dimensions={0} | all-to-all | bytes 393216 | tf_op jit(solution)/shard_map/all_to_all | solution.py:76
  168.0 13.1 %scatter_custom_fusion.4 = f32[48,257]{0,1:T(8,128)S(1)} fusion(s32[1792]{0:T(1024)S(1)} %fusion.42, f32[1792,48]{1,0:T(8,128)S(1)} %copy.401, f32[]{:T(128)} %constant.68.clone.1), kind=kCustom, calls=%fused_computation.88 | custom fusion | flops 86016 | bytes 49348 | tf_op jit(solution)/shard_map/scatter-add | solution.py:131
  181.9 37.6 %psum.97 = f32[]{:T(128)} all-reduce(f32[]{:T(128)} %get-tuple-element.23), channel_id=1, replica_groups=mesh['dom'=16,'blk'=2] {'dom','blk'}, use_global_device_ids=true, to_apply=%region_8.9 | all-reduce | flops 1 | bytes 8 | tf_op jit(solution)/shard_map/psum | solution.py:149
  223.6 33.5 %all-reduce.4 = (f32[]{:T(128)}, f32[]{:T(128)}) all-reduce(f32[]{:T(128)} %get-tuple-element.36, f32[]{:T(128)} %get-tuple-element.37), channel_id=1, replica_groups=mesh['dom'=16,'blk'=2] {'dom'}, use_global_device_ids=true, to_apply=%region_13.14 | all-reduce | flops 2 | bytes 16 | tf_op jit(solution)/shard_map/psum | solution.py:154
  264.2 18.3 %all_to_all.106 = f32[32,1,1536]{2,1,0:T(1,128)S(1)} all-to-all(f32[32,1,1536]{2,1,0:T(1,128)S(1)} %reshape.407), channel_id=1, replica_groups=mesh['dom'=16,'blk'=2] {'dom','blk'}, dimensions={0} | all-to-all | bytes 393216 | tf_op jit(solution)/shard_map/all_to_all | solution.py:81
  287.4 11.8 %convolution_bitcast_fusion.11 = f32[3,96,128]{1,0,2:T(4,128)S(1)} fusion(f32[3,96,128]{1,0,2:T(4,128)S(1)} %copy.407, f32[96,96,128]{1,0,2:T(8,128)} %copy.395), kind=kOutput, calls=%fused_computation.52 | convolution fusion | flops 42467328 | bytes 5013504 | tf_op jit(solution)/shard_map/abe,cbe->cae/dot_general | solution.py:152
  306.5 11.5 %all_to_all.107 = f32[32,1,1536]{2,1,0:T(1,128)S(1)} all-to-all(f32[32,1,1536]{2,1,0:T(1,128)S(1)} %reshape.409), channel_id=1, replica_groups=mesh['dom'=16,'blk'=2] {'dom','blk'}, dimensions={0} | all-to-all | bytes 393216 | tf_op jit(solution)/shard_map/all_to_all | solution.py:76
  319.9 13.1 %scatter_custom_fusion.6 = f32[48,257]{0,1:T(8,128)S(1)} fusion(s32[1792]{0:T(1024)S(1)} %fusion.42, f32[1792,48]{1,0:T(8,128)S(1)} %copy.414, f32[]{:T(128)} %constant.68.clone.1), kind=kCustom, calls=%fused_computation.86 | custom fusion | flops 86016 | bytes 49348 | tf_op jit(solution)/shard_map/scatter-add | solution.py:131
  336.9 31.9 %all-reduce.3 = (f32[]{:T(128)}, f32[]{:T(128)}, f32[]{:T(128)}) all-reduce(f32[]{:T(128)} %get-tuple-element.33, f32[]{:T(128)} %get-tuple-element.34, f32[]{:T(128)} %get-tuple-element.35), channel_id=1, replica_groups=mesh['dom'=16,'blk'=2] {'dom'}, use_global_device_ids=true, to_apply=%region_21.22 | all-reduce | flops 3 | bytes 24 | tf_op jit(solution)/shard_map/psum | solution.py:154
  374.2 18.2 %all_to_all.108 = f32[32,1,1536]{2,1,0:T(1,128)S(1)} all-to-all(f32[32,1,1536]{2,1,0:T(1,128)S(1)} %reshape.411), channel_id=1, replica_groups=mesh['dom'=16,'blk'=2] {'dom','blk'}, dimensions={0} | all-to-all | bytes 393216 | tf_op jit(solution)/shard_map/all_to_all | solution.py:81
  397.4 11.8 %convolution_bitcast_fusion.10 = f32[3,96,128]{1,0,2:T(4,128)S(1)} fusion(f32[3,96,128]{1,0,2:T(4,128)S(1)} %copy.420, f32[96,96,128]{1,0,2:T(8,128)} %copy.395), kind=kOutput, calls=%fused_computation.51 | convolution fusion | flops 42467328 | bytes 5013504 | tf_op jit(solution)/shard_map/abe,cbe->cae/dot_general | solution.py:152
  416.5 11.5 %all_to_all.109 = f32[32,1,1536]{2,1,0:T(1,128)S(1)} all-to-all(f32[32,1,1536]{2,1,0:T(1,128)S(1)} %reshape.413), channel_id=1, replica_groups=mesh['dom'=16,'blk'=2] {'dom','blk'}, dimensions={0} | all-to-all | bytes 393216 | tf_op jit(solution)/shard_map/all_to_all | solution.py:76
  429.9 13.1 %scatter_custom_fusion.8 = f32[48,257]{0,1:T(8,128)S(1)} fusion(s32[1792]{0:T(1024)S(1)} %fusion.42, f32[1792,48]{1,0:T(8,128)S(1)} %copy.427, f32[]{:T(128)} %constant.68.clone.1), kind=kCustom, calls=%fused_computation.84 | custom fusion | flops 86016 | bytes 49348 | tf_op jit(solution)/shard_map/scatter-add | solution.py:131
  446.8 31.9 %psum.109 = f32[]{:T(128)} all-reduce(f32[]{:T(128)} %psum.108), channel_id=1, replica_groups=mesh['dom'=16,'blk'=2] {'dom'}, use_global_device_ids=true, to_apply=%region_32.33 | all-reduce | flops 1 | bytes 8 | tf_op jit(solution)/shard_map/psum | solution.py:154
  483.4 9.7 %all-to-all-start.8 = ((f32[32,1,1536]{2,1,0:T(1,128)}), f32[32,1,1536]{2,1,0:T(1,128)S(1)}, u32[]{:S(2)}, u32[]{:S(2)}) async-start(f32[32,1,1536]{2,1,0:T(1,128)} %reshape.415), calls=%async_computation.8 | async-start | bytes 393216 | tf_op jit(solution)/shard_map/all_to_all | solution.py:81
  493.8 8.7 %all-to-all-done.8 = f32[32,1,1536]{2,1,0:T(1,128)S(1)} async-done(((f32[32,1,1536]{2,1,0:T(1,128)}), f32[32,1,1536]{2,1,0:T(1,128)S(1)}, u32[]{:S(2)}, u32[]{:S(2)}) %all-to-all-start.8) | async-done | bytes 196640 | tf_op jit(solution)/shard_map/all_to_all | solution.py:81
  507.5 8.5 %fusion.22 = f32[3,64,128]{1,0,2:T(4,128)S(1)} fusion(f32[3,64,128]{1,0,2:T(4,128)S(1)} %copy-done.4, f32[3,96,128]{1,0,2:T(4,128)S(1)} %copy.433, f32[64,96,128]{1,0,2:T(8,128)} %copy.378), kind=kOutput, calls=%fused_computation.50 | convolution fusion | flops 28336128 | bytes 3489792 | tf_op jit(solution)/shard_map/ibe,cbe->cie/dot_general | solution.py:172
  (156 shorter events, 145.8 us)
Async XLA Ops:
  0.6 22.9 %copy-start.5 = (f32[64,64,128]{2,1,0:T(8,128)S(1)}, f32[64,64,128]{2,1,0:T(8,128)}, u32[]{:S(2)}) copy-start(f32[64,64,128]{2,1,0:T(8,128)} %param.9) | copy-start | bytes 6291460
  9.6 66.6 %all-to-all-start = ((s32[32,32,1]{1,2,0:T(1,128)}), s32[32,32,1]{1,2,0:T(1,128)S(1)}, u32[]{:S(2)}, u32[]{:S(2)}) async-start(s32[32,32,1]{1,2,0:T(1,128)} %bitcast.16), calls=%async_computation | async-start | bytes 32768 | tf_op jit(solution)/shard_map/all_to_all | solution.py:114
  18.4 9.6 %copy-start.3 = (f32[3,64,128]{1,0,2:T(4,128)}, f32[3,64,128]{1,0,2:T(4,128)S(1)}, u32[]{:S(2)}) copy-start(f32[3,64,128]{1,0,2:T(4,128)S(1)} %copy.376) | copy-start | bytes 294916
  28.0 8.5 %copy-start = (f32[64,96,128]{1,0,2:T(8,128)S(1)}, f32[64,96,128]{1,0,2:T(8,128)}, u32[]{:S(2)}) copy-start(f32[64,96,128]{1,0,2:T(8,128)} %copy.378) | copy-start | bytes 9437188
  48.2 14.5 %copy-start.2 = (f32[5,16,16,1]{1,2,0,3:T(8,128)S(1)}, f32[5,16,16,1]{1,2,0,3:T(8,128)}, u32[]{:S(2)}) copy-start(f32[5,16,16,1]{1,2,0,3:T(8,128)} %constant.104) | copy-start | bytes 15364
  76.1 30.6 %copy-start.6 = (pred[257]{0:T(512)(128)(4,1)S(1)}, pred[257]{0:T(512)(128)(4,1)}, u32[]{:S(2)}) copy-start(pred[257]{0:T(512)(128)(4,1)} %constant.86.clone.1) | copy-start | bytes 775
  76.1 15.1 %all-to-all-start.1 = ((f32[32,1,1536]{2,1,0:T(1,128)}), f32[32,1,1536]{2,1,0:T(1,128)S(1)}, u32[]{:S(2)}, u32[]{:S(2)}) async-start(f32[32,1,1536]{2,1,0:T(1,128)} %reshape.401), calls=%async_computation.1 | async-start | bytes 393216 | tf_op jit(solution)/shard_map/all_to_all | solution.py:76
  110.9 15.9 %all-to-all-start.2 = ((f32[32,1,1536]{2,1,0:T(1,128)}), f32[32,1,1536]{2,1,0:T(1,128)S(1)}, u32[]{:S(2)}, u32[]{:S(2)}) async-start(f32[32,1,1536]{2,1,0:T(1,128)} %reshape.403), calls=%async_computation.2 | async-start | bytes 393216 | tf_op jit(solution)/shard_map/all_to_all | solution.py:81
  483.4 19.1 %all-to-all-start.8 = ((f32[32,1,1536]{2,1,0:T(1,128)}), f32[32,1,1536]{2,1,0:T(1,128)S(1)}, u32[]{:S(2)}, u32[]{:S(2)}) async-start(f32[32,1,1536]{2,1,0:T(1,128)} %reshape.415), calls=%async_computation.8 | async-start | bytes 393216 | tf_op jit(solution)/shard_map/all_to_all | solution.py:81
  503.9 3.6 copy-start.4
  507.5 8.5 %copy-start.1 = (f32[64,64,128]{1,0,2:T(8,128)S(1)}, f32[64,64,128]{1,0,2:T(8,128)}, u32[]{:S(2)}) copy-start(f32[64,64,128]{1,0,2:T(8,128)} %copy.377) | copy-start | bytes 6291460
